TPU v7x, 128 devices: a whole 4x4x4 slice. The times are simulated.
128 devices in a mesh: sky: 16 (over x, z), depth: 8 (over y, core).
Axes of the slice: x: 4, y: 4, z: 4, core: 2. Of those that a mesh axis runs over, the one named last changes fastest.
Arguments:
- positions: float32 [3, 2048, 128], P(None, ('sky', 'depth')), may hold values from 0 to 1
- cell_points: int32 [2048], P(('sky', 'depth')), may hold values from 1 to 128
- target_log: float32 [16], replicated, may hold values from 8 to 20
- export_count: int32 [128, 128], P(('sky', 'depth')), may hold values from 0 to 3, as said below
- export_cell: int32 [128, 128, 3], P(('sky', 'depth')), may hold values from 0 to 15
- import_pair: int32 [128, 128, 3], P(('sky', 'depth')), may hold values from 0 to 15
- import_shift: int32 [3, 128, 128, 3], P(None, ('sky', 'depth')), may hold values from -1 to 1, as said below
Outputs:
- travel: float32 [3, 2048, 128], P(None, ('sky', 'depth'))
Inputs may be any that keep to these rules, and one draw needn't show every extreme that they name: export_count[s, t] counts the slots of export_cell[s, t] that are used; it is zero unless s and t are distinct devices whose sky indices differ by at most one modulo the sky axis's size and whose depth indices differ by at most one; in every draw some device t receives 3 cells from each such neighbour. For neighbouring devices t and s, components 0 and 2 of import_shift[:, t, s, k] are the sky step and the depth step from t's region to s's region (sky taken around the cycle), component 1 varies; all components are zero for devices that are not neighbours.
All inputs are finite; a program needn't handle non-finite values.
Results may differ from a plain program's by a relative error of at most 0.00022.
Values sent between devices are 32-bit elements; how exact they have to be, the bound alone decides.
No kernel may reach another device: no remote copies, remote signals or barrier semaphores. Data moves between devices by JAX's collectives and lax.ppermute only.
A program may use at most 64 MiB of HBM per device.

v0:
```python
import jax
import jax.numpy as jnp
from jax import lax
from jax.sharding import PartitionSpec as P

STEPS = 2
EPS_SQ = 0.0001
INV_WIDTH = 16.0
STEP_SIZE = 0.01
ROW_BLOCK = 8


def from_behind(array, axis, by):
    size = lax.axis_size(axis)
    return lax.ppermute(array, axis, [(i, (i + by) % size) for i in range(size)])


def from_behind_2(value, axis, steps):
    count = lax.axis_size(axis)
    initial, last = (max(0, -steps), min(count, count - steps))
    return lax.ppermute(value, axis, [(source, source + steps) for source in range(initial, last)])


def pair_geometry(left_pos, left_mask, right_pos, right_mask, shifts, centres):
    offsets = left_pos[:, :, :, None] - right_pos[:, :, None, :] - shifts[:, :, None, None]
    radius = jnp.sqrt(jnp.sum(offsets * offsets, axis=0) + EPS_SQ)
    weight = left_mask[:, :, None] * right_mask[:, None, :]
    scaled = (radius[None] - centres[:, None, None, None]) * INV_WIDTH
    kernel = jnp.exp(-0.5 * scaled * scaled)
    return (offsets, radius, weight, scaled, kernel)


def block_counts(left_pos, left_mask, right_pos, right_mask, shifts, centres):
    offsets, radius, weight, scaled, kernel = pair_geometry(
        left_pos, left_mask, right_pos, right_mask, shifts, centres
    )
    return jnp.sum(weight[None] * kernel, axis=(1, 2, 3))


def block_forces(left_pos, left_mask, right_pos, right_mask, shifts, centres, bin_pull):
    offsets, radius, weight, scaled, kernel = pair_geometry(
        left_pos, left_mask, right_pos, right_mask, shifts, centres
    )
    slopes = jnp.sum(bin_pull[:, None, None, None] * scaled * kernel, axis=0) * -INV_WIDTH
    strength = weight * slopes / radius
    pulled = strength[None] * offsets
    return (jnp.sum(pulled, axis=3), -jnp.sum(pulled, axis=2))


def take_block(left_pos, left_mask, right_pos, right_mask, shifts, first_row):
    return (
        lax.dynamic_slice_in_dim(left_pos, first_row, ROW_BLOCK, 1),
        lax.dynamic_slice_in_dim(left_mask, first_row, ROW_BLOCK, 0),
        lax.dynamic_slice_in_dim(right_pos, first_row, ROW_BLOCK, 1),
        lax.dynamic_slice_in_dim(right_mask, first_row, ROW_BLOCK, 0),
        lax.dynamic_slice_in_dim(shifts, first_row, ROW_BLOCK, 1),
    )


def ghost_counts(left_pos, left_mask, right_pos, right_mask, shifts, centres):
    block_total = left_pos.shape[1] // ROW_BLOCK

    def add_block(block_id, running):
        pieces = take_block(
            left_pos, left_mask, right_pos, right_mask, shifts, block_id * ROW_BLOCK
        )
        return running + block_counts(
            pieces[0], pieces[1], pieces[2], pieces[3], pieces[4], centres
        )

    return lax.fori_loop(0, block_total, add_block, jnp.zeros(centres.shape, jnp.float32))


def ghost_forces(left_pos, left_mask, right_pos, right_mask, shifts, centres, bin_pull):
    block_total = left_pos.shape[1] // ROW_BLOCK

    def add_block(block_id, buffers):
        first_row = block_id * ROW_BLOCK
        pieces = take_block(left_pos, left_mask, right_pos, right_mask, shifts, first_row)
        force_left, force_right = block_forces(
            pieces[0], pieces[1], pieces[2], pieces[3], pieces[4], centres, bin_pull
        )
        return (
            lax.dynamic_update_slice_in_dim(buffers[0], force_left, first_row, 1),
            lax.dynamic_update_slice_in_dim(buffers[1], force_right, first_row, 1),
        )

    empty = jnp.zeros(left_pos.shape, jnp.float32)
    return lax.fori_loop(0, block_total, add_block, (empty, empty))


def region_offsets():
    return [
        (across, along)
        for across in (-1, 0, 1)
        for along in (-1, 0, 1)
        if (across, along) != (0, 0)
    ]


def neighbour_table():
    sky_here = lax.axis_index("sky")
    depth_here = lax.axis_index("depth")
    sky_count = lax.axis_size("sky")
    depth_count = lax.axis_size("depth")
    near_ids = []
    near_valid = []
    for across, along in region_offsets():
        depth_there = depth_here + along
        inside = (depth_there >= 0) & (depth_there < depth_count)
        clamped = jnp.clip(depth_there, 0, depth_count - 1)
        near_ids.append((sky_here + across) % sky_count * depth_count + clamped)
        near_valid.append(inside)
    return (jnp.stack(near_ids), jnp.stack(near_valid))


def near_sizes(sizes_near):
    received = [None] * 8
    for index, (across, along) in enumerate(region_offsets()):
        piece = sizes_near[index]
        if across != 0:
            piece = from_behind(piece, "sky", across)
        if along != 0:
            piece = from_behind_2(piece, "depth", along)
        received[7 - index] = piece
    return jnp.stack(received)


def near_cells(cells_near):
    received = [None] * 8
    for index, (across, along) in enumerate(region_offsets()):
        piece = cells_near[:, index]
        if across != 0:
            piece = from_behind(piece, "sky", across)
        if along != 0:
            piece = from_behind_2(piece, "depth", along)
        received[7 - index] = piece
    return jnp.stack(received, axis=1)


def near_forces(forces_near):
    received = [None] * 8
    for index, (across, along) in enumerate(region_offsets()):
        piece = forces_near[:, index]
        if across != 0:
            piece = from_behind(piece, "sky", across)
        if along != 0:
            piece = from_behind_2(piece, "depth", along)
        received[7 - index] = piece
    return jnp.stack(received, axis=1)


def send_sizes(sizes_out, near_ids, near_valid):
    return near_sizes(sizes_out[near_ids] * near_valid[:, None].astype(jnp.int32))


def send_cells(coords, export_row, near_ids):
    peer_count, slot_count = export_row.shape
    outgoing = coords[:, export_row[near_ids].reshape(-1)].reshape(
        3, 8, slot_count, coords.shape[2]
    )
    return near_cells(outgoing)


def send_forces(forces_near):
    return near_forces(forces_near)


def body(positions, cell_points, target_log, export_count, export_cell, import_pair, import_shift):
    cell_count = positions.shape[1]
    points = positions.shape[2]
    slot_count = export_cell.shape[2]
    ghosts = 8 * slot_count
    centres = (jnp.arange(target_log.shape[0], dtype=jnp.float32) + 0.5) / INV_WIDTH
    point_ids = jnp.arange(points, dtype=jnp.int32)
    point_mask = (point_ids[None, :] < cell_points[:, None]).astype(jnp.float32)
    cell_ids = jnp.arange(cell_count, dtype=jnp.int32)
    near_ids, near_valid = neighbour_table()
    live_out = jnp.arange(slot_count, dtype=jnp.int32)[None, :] < export_count[0][:, None]
    sizes_out = jnp.where(live_out, cell_points[export_cell[0]], 0)
    sizes_in = send_sizes(sizes_out, near_ids, near_valid)
    ghost_mask = (point_ids[None, :] < sizes_in.reshape(-1)[:, None]).astype(jnp.float32)
    cells_near = export_cell[0][near_ids].reshape(-1)
    live_near = (live_out[near_ids] & near_valid[:, None]).reshape(-1)
    pair_cells = import_pair[0][near_ids].reshape(-1)
    shifts = import_shift[:, 0][:, near_ids].reshape(3, ghosts).astype(jnp.float32)
    left_mask = point_mask[pair_cells]
    onehot_pair = (pair_cells[:, None] == cell_ids[None, :]).astype(jnp.float32)
    onehot_out = ((cells_near[:, None] == cell_ids[None, :]) & live_near[:, None]).astype(
        jnp.float32
    )
    zero_shift = jnp.zeros((3, cell_count), jnp.float32)
    valid_local = jnp.sum(point_mask)
    coords = positions
    travel = jnp.zeros_like(positions)
    for iteration in range(STEPS):
        ghost_pos = send_cells(coords, export_cell[0], near_ids).reshape(3, ghosts, points)
        left_pos = coords[:, pair_cells]
        self_total = block_counts(coords, point_mask, coords, point_mask, zero_shift, centres)
        ghost_total = ghost_counts(left_pos, left_mask, ghost_pos, ghost_mask, shifts, centres)
        counts = lax.psum(0.5 * self_total + ghost_total, ("sky", "depth"))
        mean_count = jnp.mean(counts)
        bin_pull = (jnp.log(1.0 + counts) - target_log) * mean_count / (1.0 + counts)
        self_grad, unused_right = block_forces(
            coords, point_mask, coords, point_mask, zero_shift, centres, bin_pull
        )
        force_left, force_right = ghost_forces(
            left_pos, left_mask, ghost_pos, ghost_mask, shifts, centres, bin_pull
        )
        returned = send_forces(force_right.reshape(3, 8, slot_count, points)).reshape(
            3, ghosts, points
        )
        gradient = self_grad
        gradient = gradient + jnp.einsum(
            "gc,kgp->kcp", onehot_pair, force_left, precision=lax.Precision.HIGHEST
        )
        gradient = gradient + jnp.einsum(
            "gc,kgp->kcp", onehot_out, returned, precision=lax.Precision.HIGHEST
        )
        power_sum, valid_count = lax.psum(
            (jnp.sum(gradient * gradient), valid_local), ("sky", "depth")
        )
        grad_rms = jnp.sqrt(power_sum / (3.0 * valid_count) + 1e-06)
        move_dir = -gradient / grad_rms
        travel = travel + move_dir
        coords = coords + STEP_SIZE * move_dir
    return travel


def solution(mesh):
    in_specs = (
        P(None, ("sky", "depth"), None),
        P(("sky", "depth")),
        P(),
        P(("sky", "depth"), None),
        P(("sky", "depth"), None, None),
        P(("sky", "depth"), None, None),
        P(None, ("sky", "depth"), None, None),
    )
    out_specs = P(None, ("sky", "depth"), None)
    return jax.shard_map(body, mesh=mesh, in_specs=in_specs, out_specs=out_specs, check_vma=False)
```

profile of v0, /device:TPU:1, one launch (start us, length us, event | category | flops | bytes accessed | tf_op | source)
XLA Modules:
  0.0 525.2 jit_solution(16160007866016866266)
XLA Ops:
  3.0 10.6 %fusion.60 = s32[128,3]{1,0:T(8,128)S(1)} fusion(s32[1,128,3]{2,1,0:T(8,128)S(1)} %copy.87, s32[]{:T(128)} %bitcast.31, s32[]{:T(128)} %bitcast.32, s32[]{:T(128)} %bitcast.33, s32[]{:T(128)} %bitcast.34, s32[]{:T(128)} %bitcast.35, s32[]{:T(128)} %bitcast.37, s32[]{:T(128)} %bitcast.36, s32[]{:T(128)} %bitcast.14, s32[]{:T(128)} %bitcast.16, s32[]{:T(128)} %bitcast.18, ...), kind=kLoop, calls=%fused_computation.175 | loop fusion | flops 13440 | bytes 3648 | tf_op jit(solution)/shard_map/jit(_where)/select_n | solution.py:180
  19.7 4.6 collective-permute-start.5
  31.1 5.1 fusion.36
  39.6 4.8 collective-permute-start.7
  47.4 5.0 collective-permute-start.17
  84.2 5.6 %collective-permute-start.20 = (f32[3,3,128]{2,1,0:T(4,128)S(1)}, f32[3,3,128]{2,1,0:T(4,128)S(1)}, u32[]{:S(2)}, u32[]{:S(2)}) collective-permute-start(f32[3,3,128]{2,1,0:T(4,128)S(1)} %collective-permute-done.19), channel_id=1, source_target_pairs={{0,1},{1,2},{2,3},{3,4},{4,5},{5,6},{6,7},{8,9},{9,10},{10,11},{11... | collective-permute-start | bytes 13832 | tf_op jit(solution)/shard_map/ppermute | solution.py:21
  94.8 10.7 %while.70 = (s32[]{:T(128)}, f32[16]{0:T(128)S(1)}, f32[24,128]{1,0:T(8,128)S(1)}, f32[24,128]{1,0:T(8,128)S(1)}, f32[3,24,128]{2,1,0:T(8,128)S(1)}, /*index=5*/...) while((s32[]{:T(128)}, f32[16]{0:T(128)S(1)}, ...), condition=%wide.region_5.6_spmd.clone, body=%wide.region_2.5_spmd.clone.sunk | while | flops 14286903 | bytes 3244889 | solution.py:71
  105.6 62.9 %psum.38 = f32[16]{0:T(128)S(1)} all-reduce(f32[16]{0:T(128)S(1)} %multiply_add_fusion.2), channel_id=1, replica_groups=mesh['sky'=16,'depth'=8] {'sky','depth'}, use_global_device_ids=true, to_apply=%region_6.7 | all-reduce | flops 16 | bytes 128 | tf_op jit(solution)/shard_map/psum | solution.py:201
  169.6 5.4 %fusion.37 = f32[16,128,128]{2,1,0:T(8,128)S(1)} fusion(f32[16]{0:T(128)S(1)} %get-tuple-element.1089, f32[16]{0:T(128)S(1)} %add_multiply_fusion.4, f32[16,128,128]{2,1,0:T(8,128)S(1)} %get-tuple-element.1163), kind=kLoop, calls=%fused_computation.105 | loop fusion | flops 29097984 | bytes 2097280 | tf_op jit(solution)/shard_map/reduce_sum | solution.py:44
  175.4 14.3 %while.68 = (s32[]{:T(128)}, f32[3,24,128]{2,1,0:T(8,128)S(1)}, f32[3,24,128]{2,1,0:T(8,128)S(1)}, f32[24,128]{1,0:T(8,128)S(1)}, f32[24,128]{1,0:T(8,128)S(1)},...) while((s32[]{:T(128)}, f32[3,24,128]{2,1,0:T(8,128)S(1)}, ...), condition=%wide.region_15.16_spmd.clone, body=%wide.region_10.0_spmd.clone.sunk | while | flops 18740276 | bytes 4916107 | solution.py:89
  203.8 4.1 collective-permute-start.31
  213.9 5.3 %collective-permute-start.32 = (f32[3,3,128]{2,1,0:T(4,128)S(1)}, f32[3,3,128]{2,1,0:T(4,128)S(1)}, u32[]{:S(2)}, u32[]{:S(2)}) collective-permute-start(f32[3,3,128]{2,1,0:T(4,128)S(1)} %collective-permute-done.31), channel_id=1, source_target_pairs={{0,1},{1,2},{2,3},{3,4},{4,5},{5,6},{6,7},{8,9},{9,10},{10,11},{11... | collective-permute-start | bytes 13832 | tf_op jit(solution)/shard_map/ppermute | solution.py:21
  225.0 62.3 %all-reduce = (f32[]{:T(128)}, f32[]{:T(128)}) all-reduce(f32[]{:T(128)} %get-tuple-element.1159, f32[]{:T(128)} %fusion.76), channel_id=1, replica_groups=mesh['sky'=16,'depth'=8] {'sky','depth'}, use_global_device_ids=true, to_apply=%region_17.18 | all-reduce | flops 2 | bytes 16 | tf_op jit(solution)/shard_map/psum | solution.py:220
  291.5 4.8 collective-permute-done.36
  296.3 4.4 collective-permute-start.37
  300.8 5.1 fusion.42
  311.0 4.8 collective-permute-start.43
  321.8 4.7 collective-permute-start.44
  331.5 10.7 %while.71 = (s32[]{:T(128)}, f32[16]{0:T(128)S(1)}, f32[24,128]{1,0:T(8,128)S(1)}, f32[24,128]{1,0:T(8,128)S(1)}, f32[3,24,128]{2,1,0:T(8,128)S(1)}, /*index=5*/...) while((s32[]{:T(128)}, f32[16]{0:T(128)S(1)}, ...), condition=%wide.region_25.26_spmd.clone, body=%wide.region_22.25_spmd.clone.sunk | while | flops 14286903 | bytes 3244889 | solution.py:71
  342.2 62.2 %psum.41 = f32[16]{0:T(128)S(1)} all-reduce(f32[16]{0:T(128)S(1)} %multiply_add_fusion.1), channel_id=1, replica_groups=mesh['sky'=16,'depth'=8] {'sky','depth'}, use_global_device_ids=true, to_apply=%region_26.27 | all-reduce | flops 16 | bytes 128 | tf_op jit(solution)/shard_map/psum | solution.py:201
  405.7 5.4 %fusion.43 = f32[16,128,128]{2,1,0:T(8,128)S(1)} fusion(f32[16]{0:T(128)S(1)} %get-tuple-element.1087, f32[16,128,128]{2,1,0:T(8,128)S(1)} %add_sqrt_fusion.4, f32[16]{0:T(128)S(1)} %add_multiply_fusion.4), kind=kLoop, calls=%fused_computation.111 | loop fusion | flops 29097984 | bytes 2097280 | tf_op jit(solution)/shard_map/reduce_sum | solution.py:44
  411.5 14.3 %while.69 = (s32[]{:T(128)}, f32[3,24,128]{2,1,0:T(8,128)S(1)}, f32[3,24,128]{2,1,0:T(8,128)S(1)}, f32[24,128]{1,0:T(8,128)S(1)}, f32[24,128]{1,0:T(8,128)S(1)},...) while((s32[]{:T(128)}, f32[3,24,128]{2,1,0:T(8,128)S(1)}, ...), condition=%wide.region_35.36_spmd.clone, body=%wide.region_30.0_spmd.clone.sunk | while | flops 18740276 | bytes 4916107 | solution.py:89
  450.2 5.3 %collective-permute-start.56 = (f32[3,3,128]{2,1,0:T(4,128)S(1)}, f32[3,3,128]{2,1,0:T(4,128)S(1)}, u32[]{:S(2)}, u32[]{:S(2)}) collective-permute-start(f32[3,3,128]{2,1,0:T(4,128)S(1)} %collective-permute-done.55), channel_id=1, source_target_pairs={{0,1},{1,2},{2,3},{3,4},{4,5},{5,6},{6,7},{8,9},{9,10},{10,11},{11... | collective-permute-start | bytes 13832 | tf_op jit(solution)/shard_map/ppermute | solution.py:21
  461.3 62.2 %psum.42 = f32[]{:T(128)} all-reduce(f32[]{:T(128)} %get-tuple-element.1161), channel_id=1, replica_groups=mesh['sky'=16,'depth'=8] {'sky','depth'}, use_global_device_ids=true, to_apply=%region_37.38 | all-reduce | flops 1 | bytes 8 | tf_op jit(solution)/shard_map/psum | solution.py:220
  (377 shorter events, 185.0 us)
Async XLA Ops:
  14.3 23.4 %collective-permute-start = (s32[3]{0:T(128)S(1)}, s32[3]{0:T(128)S(1)}, u32[]{:S(2)}, u32[]{:S(2)}) collective-permute-start(s32[3]{0:T(128)S(1)} %get-tuple-element.1142), channel_id=1, source_target_pairs={{0,8},{8,16},{16,24},{24,32},{32,40},{40,48},{48,56},{56,64},{64,7... | collective-permute-start | bytes 44 | tf_op jit(solution)/shard_map/ppermute | solution.py:15
  16.7 22.9 %collective-permute-start.2 = (s32[3]{0:T(128)S(1)}, s32[3]{0:T(128)S(1)}, u32[]{:S(2)}, u32[]{:S(2)}) collective-permute-start(s32[3]{0:T(128)S(1)} %get-tuple-element.1141), channel_id=1, source_target_pairs={{0,8},{8,16},{16,24},{24,32},{32,40},{40,48},{48,56},{56,64},{64,7... | collective-permute-start | bytes 44 | tf_op jit(solution)/shard_map/ppermute | solution.py:15
  18.4 26.1 %collective-permute-start.3 = (s32[3]{0:T(128)S(1)}, s32[3]{0:T(128)S(1)}, u32[]{:S(2)}, u32[]{:S(2)}) collective-permute-start(s32[3]{0:T(128)S(1)} %get-tuple-element.1140), channel_id=1, source_target_pairs={{0,8},{8,16},{16,24},{24,32},{32,40},{40,48},{48,56},{56,64},{64,7... | collective-permute-start | bytes 44 | tf_op jit(solution)/shard_map/ppermute | solution.py:15
  19.7 24.9 %collective-permute-start.5 = (s32[3]{0:T(128)S(1)}, s32[3]{0:T(128)S(1)}, u32[]{:S(2)}, u32[]{:S(2)}) collective-permute-start(s32[3]{0:T(128)S(1)} %get-tuple-element.1139), channel_id=1, source_target_pairs={{0,1},{1,2},{2,3},{3,4},{4,5},{5,6},{6,7},{8,9},{9,10},{10,11},{11... | collective-permute-start | bytes 44 | tf_op jit(solution)/shard_map/ppermute | solution.py:21
  26.4 44.1 %collective-permute-start.12 = (f32[3,3,128]{2,1,0:T(4,128)S(1)}, f32[3,3,128]{2,1,0:T(4,128)S(1)}, u32[]{:S(2)}, u32[]{:S(2)}) collective-permute-start(f32[3,3,128]{2,1,0:T(4,128)S(1)} %get-tuple-element.1133), channel_id=1, source_target_pairs={{0,8},{8,16},{16,24},{24,32},{32,40},{40,48},{48,56},{56,64},{64,7... | collective-permute-start | bytes 13832 | tf_op jit(solution)/shard_map/ppermute | solution.py:15
  44.7 33.7 %collective-permute-start.14 = (f32[3,3,128]{2,1,0:T(4,128)S(1)}, f32[3,3,128]{2,1,0:T(4,128)S(1)}, u32[]{:S(2)}, u32[]{:S(2)}) collective-permute-start(f32[3,3,128]{2,1,0:T(4,128)S(1)} %get-tuple-element.1132), channel_id=1, source_target_pairs={{0,8},{8,16},{16,24},{24,32},{32,40},{40,48},{48,56},{56,64},{64,7... | collective-permute-start | bytes 13832 | tf_op jit(solution)/shard_map/ppermute | solution.py:15
  46.1 33.1 %collective-permute-start.15 = (f32[3,3,128]{2,1,0:T(4,128)S(1)}, f32[3,3,128]{2,1,0:T(4,128)S(1)}, u32[]{:S(2)}, u32[]{:S(2)}) collective-permute-start(f32[3,3,128]{2,1,0:T(4,128)S(1)} %get-tuple-element.1131), channel_id=1, source_target_pairs={{0,8},{8,16},{16,24},{24,32},{32,40},{40,48},{48,56},{56,64},{64,7... | collective-permute-start | bytes 13832 | tf_op jit(solution)/shard_map/ppermute | solution.py:15
  47.4 44.3 %collective-permute-start.17 = (f32[3,3,128]{2,1,0:T(4,128)S(1)}, f32[3,3,128]{2,1,0:T(4,128)S(1)}, u32[]{:S(2)}, u32[]{:S(2)}) collective-permute-start(f32[3,3,128]{2,1,0:T(4,128)S(1)} %get-tuple-element.1130), channel_id=1, source_target_pairs={{0,1},{1,2},{2,3},{3,4},{4,5},{5,6},{6,7},{8,9},{9,10},{10,11},{11... | collective-permute-start | bytes 13832 | tf_op jit(solution)/shard_map/ppermute | solution.py:21
  68.5 23.3 %collective-permute-start.18 = (f32[3,3,128]{2,1,0:T(4,128)S(1)}, f32[3,3,128]{2,1,0:T(4,128)S(1)}, u32[]{:S(2)}, u32[]{:S(2)}) collective-permute-start(f32[3,3,128]{2,1,0:T(4,128)S(1)} %get-tuple-element.1129), channel_id=1, source_target_pairs={{1,0},{2,1},{3,2},{4,3},{5,4},{6,5},{7,6},{9,8},{10,9},{11,10},{12... | collective-permute-start | bytes 13832 | tf_op jit(solution)/shard_map/ppermute | solution.py:21
  192.2 15.6 %collective-permute-start.26 = (f32[3,3,128]{2,1,0:T(4,128)S(1)}, f32[3,3,128]{2,1,0:T(4,128)S(1)}, u32[]{:S(2)}, u32[]{:S(2)}) collective-permute-start(f32[3,3,128]{2,1,0:T(4,128)S(1)} %get-tuple-element.1124), channel_id=1, source_target_pairs={{0,8},{8,16},{16,24},{24,32},{32,40},{40,48},{48,56},{56,64},{64,7... | collective-permute-start | bytes 13832 | tf_op jit(solution)/shard_map/ppermute | solution.py:15
  192.6 15.6 %collective-permute-start.27 = (f32[3,3,128]{2,1,0:T(4,128)S(1)}, f32[3,3,128]{2,1,0:T(4,128)S(1)}, u32[]{:S(2)}, u32[]{:S(2)}) collective-permute-start(f32[3,3,128]{2,1,0:T(4,128)S(1)} %get-tuple-element.1123), channel_id=1, source_target_pairs={{0,8},{8,16},{16,24},{24,32},{32,40},{40,48},{48,56},{56,64},{64,7... | collective-permute-start | bytes 13832 | tf_op jit(solution)/shard_map/ppermute | solution.py:15
  194.3 26.9 %collective-permute-start.29 = (f32[3,3,128]{2,1,0:T(4,128)S(1)}, f32[3,3,128]{2,1,0:T(4,128)S(1)}, u32[]{:S(2)}, u32[]{:S(2)}) collective-permute-start(f32[3,3,128]{2,1,0:T(4,128)S(1)} %get-tuple-element.1122), channel_id=1, source_target_pairs={{0,1},{1,2},{2,3},{3,4},{4,5},{5,6},{6,7},{8,9},{9,10},{10,11},{11... | collective-permute-start | bytes 13832 | tf_op jit(solution)/shard_map/ppermute | solution.py:21
  197.4 23.8 %collective-permute-start.30 = (f32[3,3,128]{2,1,0:T(4,128)S(1)}, f32[3,3,128]{2,1,0:T(4,128)S(1)}, u32[]{:S(2)}, u32[]{:S(2)}) collective-permute-start(f32[3,3,128]{2,1,0:T(4,128)S(1)} %get-tuple-element.1121), channel_id=1, source_target_pairs={{1,0},{2,1},{3,2},{4,3},{5,4},{6,5},{7,6},{9,8},{10,9},{11,10},{12... | collective-permute-start | bytes 13832 | tf_op jit(solution)/shard_map/ppermute | solution.py:21
  208.2 11.0 %collective-permute-start.28 = (f32[3,3,128]{2,1,0:T(4,128)S(1)}, f32[3,3,128]{2,1,0:T(4,128)S(1)}, u32[]{:S(2)}, u32[]{:S(2)}) collective-permute-start(f32[3,3,128]{2,1,0:T(4,128)S(1)} %collective-permute-done.27), channel_id=1, source_target_pairs={{1,0},{2,1},{3,2},{4,3},{5,4},{6,5},{7,6},{9,8},{10,9},{11,10},{12... | collective-permute-start | bytes 13832 | tf_op jit(solution)/shard_map/ppermute | solution.py:21
  210.2 11.1 %collective-permute-start.33 = (f32[3,3,128]{2,1,0:T(4,128)S(1)}, f32[3,3,128]{2,1,0:T(4,128)S(1)}, u32[]{:S(2)}, u32[]{:S(2)}) collective-permute-start(f32[3,3,128]{2,1,0:T(4,128)S(1)} %get-tuple-element.1126), channel_id=1, source_target_pairs={{0,120},{8,0},{16,8},{24,16},{32,24},{40,32},{48,40},{56,48},{64,5... | collective-permute-start | bytes 13832 | tf_op jit(solution)/shard_map/ppermute | solution.py:15
  296.3 14.7 %collective-permute-start.37 = (f32[3,3,128]{2,1,0:T(4,128)S(1)}, f32[3,3,128]{2,1,0:T(4,128)S(1)}, u32[]{:S(2)}, u32[]{:S(2)}) collective-permute-start(f32[3,3,128]{2,1,0:T(4,128)S(1)} %collective-permute-done.36), channel_id=1, source_target_pairs={{0,1},{1,2},{2,3},{3,4},{4,5},{5,6},{6,7},{8,9},{9,10},{10,11},{11... | collective-permute-start | bytes 13832 | tf_op jit(solution)/shard_map/ppermute | solution.py:21
  306.6 21.8 %collective-permute-start.41 = (f32[3,3,128]{2,1,0:T(4,128)S(1)}, f32[3,3,128]{2,1,0:T(4,128)S(1)}, u32[]{:S(2)}, u32[]{:S(2)}) collective-permute-start(f32[3,3,128]{2,1,0:T(4,128)S(1)} %bitcast.330), channel_id=1, source_target_pairs={{0,1},{1,2},{2,3},{3,4},{4,5},{5,6},{6,7},{8,9},{9,10},{10,11},{11... | collective-permute-start | bytes 13832 | tf_op jit(solution)/shard_map/ppermute | solution.py:21
  308.6 19.9 %collective-permute-start.42 = (f32[3,3,128]{2,1,0:T(4,128)S(1)}, f32[3,3,128]{2,1,0:T(4,128)S(1)}, u32[]{:S(2)}, u32[]{:S(2)}) collective-permute-start(f32[3,3,128]{2,1,0:T(4,128)S(1)} %bitcast.329), channel_id=1, source_target_pairs={{1,0},{2,1},{3,2},{4,3},{5,4},{6,5},{7,6},{9,8},{10,9},{11,10},{12... | collective-permute-start | bytes 13832 | tf_op jit(solution)/shard_map/ppermute | solution.py:21
  428.5 15.6 %collective-permute-start.50 = (f32[3,3,128]{2,1,0:T(4,128)S(1)}, f32[3,3,128]{2,1,0:T(4,128)S(1)}, u32[]{:S(2)}, u32[]{:S(2)}) collective-permute-start(f32[3,3,128]{2,1,0:T(4,128)S(1)} %get-tuple-element.1108), channel_id=1, source_target_pairs={{0,8},{8,16},{16,24},{24,32},{32,40},{40,48},{48,56},{56,64},{64,7... | collective-permute-start | bytes 13832 | tf_op jit(solution)/shard_map/ppermute | solution.py:15
  428.7 15.9 %collective-permute-start.51 = (f32[3,3,128]{2,1,0:T(4,128)S(1)}, f32[3,3,128]{2,1,0:T(4,128)S(1)}, u32[]{:S(2)}, u32[]{:S(2)}) collective-permute-start(f32[3,3,128]{2,1,0:T(4,128)S(1)} %get-tuple-element.1107), channel_id=1, source_target_pairs={{0,8},{8,16},{16,24},{24,32},{32,40},{40,48},{48,56},{56,64},{64,7... | collective-permute-start | bytes 13832 | tf_op jit(solution)/shard_map/ppermute | solution.py:15
  430.7 26.9 %collective-permute-start.53 = (f32[3,3,128]{2,1,0:T(4,128)S(1)}, f32[3,3,128]{2,1,0:T(4,128)S(1)}, u32[]{:S(2)}, u32[]{:S(2)}) collective-permute-start(f32[3,3,128]{2,1,0:T(4,128)S(1)} %get-tuple-element.1106), channel_id=1, source_target_pairs={{0,1},{1,2},{2,3},{3,4},{4,5},{5,6},{6,7},{8,9},{9,10},{10,11},{11... | collective-permute-start | bytes 13832 | tf_op jit(solution)/shard_map/ppermute | solution.py:21
  434.0 23.5 %collective-permute-start.54 = (f32[3,3,128]{2,1,0:T(4,128)S(1)}, f32[3,3,128]{2,1,0:T(4,128)S(1)}, u32[]{:S(2)}, u32[]{:S(2)}) collective-permute-start(f32[3,3,128]{2,1,0:T(4,128)S(1)} %get-tuple-element.1105), channel_id=1, source_target_pairs={{1,0},{2,1},{3,2},{4,3},{5,4},{6,5},{7,6},{9,8},{10,9},{11,10},{12... | collective-permute-start | bytes 13832 | tf_op jit(solution)/shard_map/ppermute | solution.py:21
  444.6 10.9 %collective-permute-start.52 = (f32[3,3,128]{2,1,0:T(4,128)S(1)}, f32[3,3,128]{2,1,0:T(4,128)S(1)}, u32[]{:S(2)}, u32[]{:S(2)}) collective-permute-start(f32[3,3,128]{2,1,0:T(4,128)S(1)} %collective-permute-done.51), channel_id=1, source_target_pairs={{1,0},{2,1},{3,2},{4,3},{5,4},{6,5},{7,6},{9,8},{10,9},{11,10},{12... | collective-permute-start | bytes 13832 | tf_op jit(solution)/shard_map/ppermute | solution.py:21
  446.6 11.0 %collective-permute-start.57 = (f32[3,3,128]{2,1,0:T(4,128)S(1)}, f32[3,3,128]{2,1,0:T(4,128)S(1)}, u32[]{:S(2)}, u32[]{:S(2)}) collective-permute-start(f32[3,3,128]{2,1,0:T(4,128)S(1)} %get-tuple-element.1110), channel_id=1, source_target_pairs={{0,120},{8,0},{16,8},{24,16},{32,24},{40,32},{48,40},{56,48},{64,5... | collective-permute-start | bytes 13832 | tf_op jit(solution)/shard_map/ppermute | solution.py:15
  (42 other events, 449.1 us)
where the time goes:
time: 535 us; the launch traced here: 525 us
  blocking collectives  250 us (47%)
  starting transfers between devices  140 us (26%)
  other arithmetic  89.7 us (17%)
  waiting for transfers between devices  26.4 us (5%)
  local copies, waits for them, and re-layouts  12.1 us (2%)
    psum x2, blocking collectives, body(): counts = lax.psum(0.5 * self_total + ghost_total, ('sky', 'depth'))  125 us
    psum x2, blocking collectives, body(): lax.psum((jnp.sum(gradient * gradient), valid_local), ('sky', 'depth'))  124 us
    ppermute x30, starting transfers between devices, from_behind_2(): lax.ppermute(value, axis, [(source, source + steps) for source in range(i...  87.8 us
    ppermute x30, starting transfers between devices, from_behind(): lax.ppermute(array, axis, [(i, (i + by) % size) for i in range(size)])  52.4 us
    reduce_sum x8, other arithmetic, block_forces(): jnp.sum(bin_pull[:, None, None, None] * scaled * kernel, axis=0)  26.9 us
    reduce_sum x8, other arithmetic, block_counts(): return jnp.sum(weight[None] * kernel, axis=(1, 2, 3))  25.4 us
    ppermute x30, waiting for transfers between devices, from_behind_2(): lax.ppermute(value, axis, [(source, source + steps) for source in range(i...  21.5 us
  transfers between devices with their start and end apart: 60, of which 12 were waited for; matrix products, arithmetic and copies ran while one was open for 4% of the time, Pallas kernels for 0%

commit v1 on v0

--- a/solution.py
+++ b/solution.py
@@ -198,7 +198,7 @@
         left_pos = coords[:, pair_cells]
         self_total = block_counts(coords, point_mask, coords, point_mask, zero_shift, centres)
         ghost_total = ghost_counts(left_pos, left_mask, ghost_pos, ghost_mask, shifts, centres)
-        counts = lax.psum(0.5 * self_total + ghost_total, ("sky", "depth"))
+        counts = lax.psum(lax.psum(0.5 * self_total + ghost_total, "depth"), "sky")
         mean_count = jnp.mean(counts)
         bin_pull = (jnp.log(1.0 + counts) - target_log) * mean_count / (1.0 + counts)
         self_grad, unused_right = block_forces(

time: 535 us -> 504 us (0.942)
  blocking collectives: 250 us -> 206 us
  starting transfers between devices: 140 us -> 152 us
    psum x2 -> x4, blocking collectives: 125 us -> 81.4 us  [body(): counts = lax.psum(lax.psum(0.5 * self_total + ghost_total, 'depth'), 'sky')]
    ppermute x30, starting transfers between devices: 87.8 us -> 102 us  [from_behind_2(): lax.ppermute(value, axis, [(source, source + steps) for source in range(i...]
  transfers between devices with their start and end apart: 60 -> 60, of which waited for: 12 -> 12; matrix products, arithmetic and copies ran while one was open for 4% -> 5% of each run, Pallas kernels for 0% -> 0%
where the time goes in v1:
time: 504 us; the launch traced here: 494 us
  blocking collectives  206 us (41%)
  starting transfers between devices  152 us (30%)
  other arithmetic  89.9 us (18%)
  waiting for transfers between devices  26.5 us (5%)
  local copies, waits for them, and re-layouts  12.1 us (2%)
    psum x2, blocking collectives, body(): lax.psum((jnp.sum(gradient * gradient), valid_local), ('sky', 'depth'))  125 us
    ppermute x30, starting transfers between devices, from_behind_2(): lax.ppermute(value, axis, [(source, source + steps) for source in range(i...  102 us
    psum x4, blocking collectives, body(): counts = lax.psum(lax.psum(0.5 * self_total + ghost_total, 'depth'), 'sky')  81.4 us
    ppermute x30, starting transfers between devices, from_behind(): lax.ppermute(array, axis, [(i, (i + by) % size) for i in range(size)])  49.6 us
    reduce_sum x8, other arithmetic, block_forces(): jnp.sum(bin_pull[:, None, None, None] * scaled * kernel, axis=0)  26.9 us
    reduce_sum x8, other arithmetic, block_counts(): return jnp.sum(weight[None] * kernel, axis=(1, 2, 3))  25.4 us
    ppermute x30, waiting for transfers between devices, from_behind_2(): lax.ppermute(value, axis, [(source, source + steps) for source in range(i...  21.5 us
    select_n x1, other arithmetic, body(): sizes_out = jnp.where(live_out, cell_points[export_cell[0]], 0)  10.7 us
  transfers between devices with their start and end apart: 60, of which 12 were waited for; matrix products, arithmetic and copies ran while one was open for 5% of the time, Pallas kernels for 0%

profile of v1, /device:TPU:1, one launch (start us, length us, event | category | flops | bytes accessed | tf_op | source)
XLA Modules:
  0.0 494.3 jit_solution(8473176873060150616)
XLA Ops:
  3.0 10.7 %fusion.60 = s32[128,3]{1,0:T(8,128)S(1)} fusion(s32[1,128,3]{2,1,0:T(8,128)S(1)} %copy.87, s32[]{:T(128)} %bitcast.31, s32[]{:T(128)} %bitcast.32, s32[]{:T(128)} %bitcast.33, s32[]{:T(128)} %bitcast.34, s32[]{:T(128)} %bitcast.35, s32[]{:T(128)} %bitcast.37, s32[]{:T(128)} %bitcast.36, s32[]{:T(128)} %bitcast.14, s32[]{:T(128)} %bitcast.16, s32[]{:T(128)} %bitcast.18, ...), kind=kLoop, calls=%fused_computation.175 | loop fusion | flops 13440 | bytes 3648 | tf_op jit(solution)/shard_map/jit(_where)/select_n | solution.py:180
  31.3 5.1 %fusion.36 = f32[16]{0:T(128)S(1)} fusion(f32[16,128,128]{2,1,0:T(8,128)S(1)} %get-tuple-element.1164, f32[16]{0:T(128)S(1)} %add_multiply_fusion.4, f32[16,128,128]{2,1,0:T(8,128)S(1)} %get-tuple-element.1163), kind=kLoop, calls=%fused_computation.104 | loop fusion | flops 25165808 | bytes 2097280 | tf_op jit(solution)/shard_map/reduce_sum | solution.py:37
  47.5 5.0 %collective-permute-start.17 = (f32[3,3,128]{2,1,0:T(4,128)S(1)}, f32[3,3,128]{2,1,0:T(4,128)S(1)}, u32[]{:S(2)}, u32[]{:S(2)}) collective-permute-start(f32[3,3,128]{2,1,0:T(4,128)S(1)} %get-tuple-element.1130), channel_id=1, source_target_pairs={{0,1},{1,2},{2,3},{3,4},{4,5},{5,6},{6,7},{8,9},{9,10},{10,11},{11... | collective-permute-start | bytes 13832 | tf_op jit(solution)/shard_map/ppermute | solution.py:21
  84.3 5.6 %collective-permute-start.20 = (f32[3,3,128]{2,1,0:T(4,128)S(1)}, f32[3,3,128]{2,1,0:T(4,128)S(1)}, u32[]{:S(2)}, u32[]{:S(2)}) collective-permute-start(f32[3,3,128]{2,1,0:T(4,128)S(1)} %collective-permute-done.19), channel_id=1, source_target_pairs={{0,1},{1,2},{2,3},{3,4},{4,5},{5,6},{6,7},{8,9},{9,10},{10,11},{11... | collective-permute-start | bytes 13832 | tf_op jit(solution)/shard_map/ppermute | solution.py:21
  94.9 10.7 %while.70 = (s32[]{:T(128)}, f32[16]{0:T(128)S(1)}, f32[24,128]{1,0:T(8,128)S(1)}, f32[24,128]{1,0:T(8,128)S(1)}, f32[3,24,128]{2,1,0:T(8,128)S(1)}, /*index=5*/...) while((s32[]{:T(128)}, f32[16]{0:T(128)S(1)}, ...), condition=%wide.region_5.6_spmd.clone, body=%wide.region_2.5_spmd.clone.sunk | while | flops 14286903 | bytes 3244889 | solution.py:71
  105.6 10.8 %psum.52 = f32[16]{0:T(128)S(1)} all-reduce(f32[16]{0:T(128)S(1)} %multiply_add_fusion.2), channel_id=1, replica_groups=mesh['sky'=16,'depth'=8] {'depth'}, use_global_device_ids=true, to_apply=%region_6.7 | all-reduce | flops 16 | bytes 128 | tf_op jit(solution)/shard_map/psum | solution.py:201
  116.5 29.8 %psum.53 = f32[16]{0:T(128)S(1)} all-reduce(f32[16]{0:T(128)S(1)} %psum.52), channel_id=1, replica_groups=mesh['sky'=16,'depth'=8] {'sky'}, use_global_device_ids=true, to_apply=%region_7.8 | all-reduce | flops 16 | bytes 128 | tf_op jit(solution)/shard_map/psum | solution.py:201
  147.6 5.4 %fusion.37 = f32[16,128,128]{2,1,0:T(8,128)S(1)} fusion(f32[16]{0:T(128)S(1)} %get-tuple-element.1089, f32[16]{0:T(128)S(1)} %add_multiply_fusion.4, f32[16,128,128]{2,1,0:T(8,128)S(1)} %get-tuple-element.1163), kind=kLoop, calls=%fused_computation.105 | loop fusion | flops 29097984 | bytes 2097280 | tf_op jit(solution)/shard_map/reduce_sum | solution.py:44
  153.3 14.3 %while.68 = (s32[]{:T(128)}, f32[3,24,128]{2,1,0:T(8,128)S(1)}, f32[3,24,128]{2,1,0:T(8,128)S(1)}, f32[24,128]{1,0:T(8,128)S(1)}, f32[24,128]{1,0:T(8,128)S(1)},...) while((s32[]{:T(128)}, f32[3,24,128]{2,1,0:T(8,128)S(1)}, ...), condition=%wide.region_16.17_spmd.clone, body=%wide.region_11.0_spmd.clone.sunk | while | flops 18740276 | bytes 4916107 | solution.py:89
  170.5 10.3 %collective-permute-start.29 = (f32[3,3,128]{2,1,0:T(4,128)S(1)}, f32[3,3,128]{2,1,0:T(4,128)S(1)}, u32[]{:S(2)}, u32[]{:S(2)}) collective-permute-start(f32[3,3,128]{2,1,0:T(4,128)S(1)} %get-tuple-element.1122), channel_id=1, source_target_pairs={{0,1},{1,2},{2,3},{3,4},{4,5},{5,6},{6,7},{8,9},{9,10},{10,11},{11... | collective-permute-start | bytes 13832 | tf_op jit(solution)/shard_map/ppermute | solution.py:21
  187.1 5.0 %collective-permute-start.31 = (f32[3,3,128]{2,1,0:T(4,128)S(1)}, f32[3,3,128]{2,1,0:T(4,128)S(1)}, u32[]{:S(2)}, u32[]{:S(2)}) collective-permute-start(f32[3,3,128]{2,1,0:T(4,128)S(1)} %get-tuple-element.1120), channel_id=1, source_target_pairs={{0,120},{8,0},{16,8},{24,16},{32,24},{40,32},{48,40},{56,48},{64,5... | collective-permute-start | bytes 13832 | tf_op jit(solution)/shard_map/ppermute | solution.py:15
  198.1 5.5 %collective-permute-start.32 = (f32[3,3,128]{2,1,0:T(4,128)S(1)}, f32[3,3,128]{2,1,0:T(4,128)S(1)}, u32[]{:S(2)}, u32[]{:S(2)}) collective-permute-start(f32[3,3,128]{2,1,0:T(4,128)S(1)} %collective-permute-done.31), channel_id=1, source_target_pairs={{0,1},{1,2},{2,3},{3,4},{4,5},{5,6},{6,7},{8,9},{9,10},{10,11},{11... | collective-permute-start | bytes 13832 | tf_op jit(solution)/shard_map/ppermute | solution.py:21
  209.4 62.8 %all-reduce = (f32[]{:T(128)}, f32[]{:T(128)}) all-reduce(f32[]{:T(128)} %get-tuple-element.1159, f32[]{:T(128)} %fusion.76), channel_id=1, replica_groups=mesh['sky'=16,'depth'=8] {'sky','depth'}, use_global_device_ids=true, to_apply=%region_18.19 | all-reduce | flops 2 | bytes 16 | tf_op jit(solution)/shard_map/psum | solution.py:220
  276.2 4.9 collective-permute-done.36
  285.6 5.1 %fusion.42 = f32[16]{0:T(128)S(1)} fusion(f32[16,128,128]{2,1,0:T(8,128)S(1)} %add_sqrt_fusion.4, f32[16,128,128]{2,1,0:T(8,128)S(1)} %get-tuple-element.1164, f32[16]{0:T(128)S(1)} %add_multiply_fusion.4), kind=kLoop, calls=%fused_computation.110 | loop fusion | flops 25165808 | bytes 2097280 | tf_op jit(solution)/shard_map/reduce_sum | solution.py:37
  316.4 10.7 %while.71 = (s32[]{:T(128)}, f32[16]{0:T(128)S(1)}, f32[24,128]{1,0:T(8,128)S(1)}, f32[24,128]{1,0:T(8,128)S(1)}, f32[3,24,128]{2,1,0:T(8,128)S(1)}, /*index=5*/...) while((s32[]{:T(128)}, f32[16]{0:T(128)S(1)}, ...), condition=%wide.region_26.27_spmd.clone, body=%wide.region_23.26_spmd.clone.sunk | while | flops 14286903 | bytes 3244889 | solution.py:71
  327.1 10.7 %psum.56 = f32[16]{0:T(128)S(1)} all-reduce(f32[16]{0:T(128)S(1)} %multiply_add_fusion.1), channel_id=1, replica_groups=mesh['sky'=16,'depth'=8] {'depth'}, use_global_device_ids=true, to_apply=%region_27.28 | all-reduce | flops 16 | bytes 128 | tf_op jit(solution)/shard_map/psum | solution.py:201
  337.7 30.1 %psum.57 = f32[16]{0:T(128)S(1)} all-reduce(f32[16]{0:T(128)S(1)} %psum.56), channel_id=1, replica_groups=mesh['sky'=16,'depth'=8] {'sky'}, use_global_device_ids=true, to_apply=%region_28.29 | all-reduce | flops 16 | bytes 128 | tf_op jit(solution)/shard_map/psum | solution.py:201
  369.1 5.4 %fusion.43 = f32[16,128,128]{2,1,0:T(8,128)S(1)} fusion(f32[16]{0:T(128)S(1)} %get-tuple-element.1087, f32[16,128,128]{2,1,0:T(8,128)S(1)} %add_sqrt_fusion.4, f32[16]{0:T(128)S(1)} %add_multiply_fusion.4), kind=kLoop, calls=%fused_computation.111 | loop fusion | flops 29097984 | bytes 2097280 | tf_op jit(solution)/shard_map/reduce_sum | solution.py:44
  374.9 14.3 %while.69 = (s32[]{:T(128)}, f32[3,24,128]{2,1,0:T(8,128)S(1)}, f32[3,24,128]{2,1,0:T(8,128)S(1)}, f32[24,128]{1,0:T(8,128)S(1)}, f32[24,128]{1,0:T(8,128)S(1)},...) while((s32[]{:T(128)}, f32[3,24,128]{2,1,0:T(8,128)S(1)}, ...), condition=%wide.region_37.38_spmd.clone, body=%wide.region_32.0_spmd.clone.sunk | while | flops 18740276 | bytes 4916107 | solution.py:89
  391.6 10.3 %collective-permute-start.53 = (f32[3,3,128]{2,1,0:T(4,128)S(1)}, f32[3,3,128]{2,1,0:T(4,128)S(1)}, u32[]{:S(2)}, u32[]{:S(2)}) collective-permute-start(f32[3,3,128]{2,1,0:T(4,128)S(1)} %get-tuple-element.1106), channel_id=1, source_target_pairs={{0,1},{1,2},{2,3},{3,4},{4,5},{5,6},{6,7},{8,9},{9,10},{10,11},{11... | collective-permute-start | bytes 13832 | tf_op jit(solution)/shard_map/ppermute | solution.py:21
  408.2 5.0 %collective-permute-start.55 = (f32[3,3,128]{2,1,0:T(4,128)S(1)}, f32[3,3,128]{2,1,0:T(4,128)S(1)}, u32[]{:S(2)}, u32[]{:S(2)}) collective-permute-start(f32[3,3,128]{2,1,0:T(4,128)S(1)} %get-tuple-element.1104), channel_id=1, source_target_pairs={{0,120},{8,0},{16,8},{24,16},{32,24},{40,32},{48,40},{56,48},{64,5... | collective-permute-start | bytes 13832 | tf_op jit(solution)/shard_map/ppermute | solution.py:15
  419.2 5.5 %collective-permute-start.56 = (f32[3,3,128]{2,1,0:T(4,128)S(1)}, f32[3,3,128]{2,1,0:T(4,128)S(1)}, u32[]{:S(2)}, u32[]{:S(2)}) collective-permute-start(f32[3,3,128]{2,1,0:T(4,128)S(1)} %collective-permute-done.55), channel_id=1, source_target_pairs={{0,1},{1,2},{2,3},{3,4},{4,5},{5,6},{6,7},{8,9},{9,10},{10,11},{11... | collective-permute-start | bytes 13832 | tf_op jit(solution)/shard_map/ppermute | solution.py:21
  430.4 62.4 %psum.58 = f32[]{:T(128)} all-reduce(f32[]{:T(128)} %get-tuple-element.1161), channel_id=1, replica_groups=mesh['sky'=16,'depth'=8] {'sky','depth'}, use_global_device_ids=true, to_apply=%region_39.40 | all-reduce | flops 1 | bytes 8 | tf_op jit(solution)/shard_map/psum | solution.py:220
  (379 shorter events, 193.4 us)
Async XLA Ops:
  14.3 23.5 %collective-permute-start = (s32[3]{0:T(128)S(1)}, s32[3]{0:T(128)S(1)}, u32[]{:S(2)}, u32[]{:S(2)}) collective-permute-start(s32[3]{0:T(128)S(1)} %get-tuple-element.1142), channel_id=1, source_target_pairs={{0,8},{8,16},{16,24},{24,32},{32,40},{40,48},{48,56},{56,64},{64,7... | collective-permute-start | bytes 44 | tf_op jit(solution)/shard_map/ppermute | solution.py:15
  16.8 22.9 %collective-permute-start.2 = (s32[3]{0:T(128)S(1)}, s32[3]{0:T(128)S(1)}, u32[]{:S(2)}, u32[]{:S(2)}) collective-permute-start(s32[3]{0:T(128)S(1)} %get-tuple-element.1141), channel_id=1, source_target_pairs={{0,8},{8,16},{16,24},{24,32},{32,40},{40,48},{48,56},{56,64},{64,7... | collective-permute-start | bytes 44 | tf_op jit(solution)/shard_map/ppermute | solution.py:15
  18.5 26.1 %collective-permute-start.3 = (s32[3]{0:T(128)S(1)}, s32[3]{0:T(128)S(1)}, u32[]{:S(2)}, u32[]{:S(2)}) collective-permute-start(s32[3]{0:T(128)S(1)} %get-tuple-element.1140), channel_id=1, source_target_pairs={{0,8},{8,16},{16,24},{24,32},{32,40},{40,48},{48,56},{56,64},{64,7... | collective-permute-start | bytes 44 | tf_op jit(solution)/shard_map/ppermute | solution.py:15
  19.8 24.9 %collective-permute-start.5 = (s32[3]{0:T(128)S(1)}, s32[3]{0:T(128)S(1)}, u32[]{:S(2)}, u32[]{:S(2)}) collective-permute-start(s32[3]{0:T(128)S(1)} %get-tuple-element.1139), channel_id=1, source_target_pairs={{0,1},{1,2},{2,3},{3,4},{4,5},{5,6},{6,7},{8,9},{9,10},{10,11},{11... | collective-permute-start | bytes 44 | tf_op jit(solution)/shard_map/ppermute | solution.py:21
  26.5 44.2 %collective-permute-start.12 = (f32[3,3,128]{2,1,0:T(4,128)S(1)}, f32[3,3,128]{2,1,0:T(4,128)S(1)}, u32[]{:S(2)}, u32[]{:S(2)}) collective-permute-start(f32[3,3,128]{2,1,0:T(4,128)S(1)} %get-tuple-element.1133), channel_id=1, source_target_pairs={{0,8},{8,16},{16,24},{24,32},{32,40},{40,48},{48,56},{56,64},{64,7... | collective-permute-start | bytes 13832 | tf_op jit(solution)/shard_map/ppermute | solution.py:15
  44.8 33.7 %collective-permute-start.14 = (f32[3,3,128]{2,1,0:T(4,128)S(1)}, f32[3,3,128]{2,1,0:T(4,128)S(1)}, u32[]{:S(2)}, u32[]{:S(2)}) collective-permute-start(f32[3,3,128]{2,1,0:T(4,128)S(1)} %get-tuple-element.1132), channel_id=1, source_target_pairs={{0,8},{8,16},{16,24},{24,32},{32,40},{40,48},{48,56},{56,64},{64,7... | collective-permute-start | bytes 13832 | tf_op jit(solution)/shard_map/ppermute | solution.py:15
  46.2 33.1 %collective-permute-start.15 = (f32[3,3,128]{2,1,0:T(4,128)S(1)}, f32[3,3,128]{2,1,0:T(4,128)S(1)}, u32[]{:S(2)}, u32[]{:S(2)}) collective-permute-start(f32[3,3,128]{2,1,0:T(4,128)S(1)} %get-tuple-element.1131), channel_id=1, source_target_pairs={{0,8},{8,16},{16,24},{24,32},{32,40},{40,48},{48,56},{56,64},{64,7... | collective-permute-start | bytes 13832 | tf_op jit(solution)/shard_map/ppermute | solution.py:15
  47.5 44.3 %collective-permute-start.17 = (f32[3,3,128]{2,1,0:T(4,128)S(1)}, f32[3,3,128]{2,1,0:T(4,128)S(1)}, u32[]{:S(2)}, u32[]{:S(2)}) collective-permute-start(f32[3,3,128]{2,1,0:T(4,128)S(1)} %get-tuple-element.1130), channel_id=1, source_target_pairs={{0,1},{1,2},{2,3},{3,4},{4,5},{5,6},{6,7},{8,9},{9,10},{10,11},{11... | collective-permute-start | bytes 13832 | tf_op jit(solution)/shard_map/ppermute | solution.py:21
  68.6 23.3 %collective-permute-start.18 = (f32[3,3,128]{2,1,0:T(4,128)S(1)}, f32[3,3,128]{2,1,0:T(4,128)S(1)}, u32[]{:S(2)}, u32[]{:S(2)}) collective-permute-start(f32[3,3,128]{2,1,0:T(4,128)S(1)} %get-tuple-element.1129), channel_id=1, source_target_pairs={{1,0},{2,1},{3,2},{4,3},{5,4},{6,5},{7,6},{9,8},{10,9},{11,10},{12... | collective-permute-start | bytes 13832 | tf_op jit(solution)/shard_map/ppermute | solution.py:21
  81.3 10.7 %collective-permute-start.21 = (f32[3,3,128]{2,1,0:T(4,128)S(1)}, f32[3,3,128]{2,1,0:T(4,128)S(1)}, u32[]{:S(2)}, u32[]{:S(2)}) collective-permute-start(f32[3,3,128]{2,1,0:T(4,128)S(1)} %get-tuple-element.1134), channel_id=1, source_target_pairs={{0,120},{8,0},{16,8},{24,16},{32,24},{40,32},{48,40},{56,48},{64,5... | collective-permute-start | bytes 13832 | tf_op jit(solution)/shard_map/ppermute | solution.py:15
  167.7 15.6 %collective-permute-start.24 = (f32[3,3,128]{2,1,0:T(4,128)S(1)}, f32[3,3,128]{2,1,0:T(4,128)S(1)}, u32[]{:S(2)}, u32[]{:S(2)}) collective-permute-start(f32[3,3,128]{2,1,0:T(4,128)S(1)} %get-tuple-element.1125), channel_id=1, source_target_pairs={{0,8},{8,16},{16,24},{24,32},{32,40},{40,48},{48,56},{56,64},{64,7... | collective-permute-start | bytes 13832 | tf_op jit(solution)/shard_map/ppermute | solution.py:15
  170.3 21.9 %collective-permute-start.26 = (f32[3,3,128]{2,1,0:T(4,128)S(1)}, f32[3,3,128]{2,1,0:T(4,128)S(1)}, u32[]{:S(2)}, u32[]{:S(2)}) collective-permute-start(f32[3,3,128]{2,1,0:T(4,128)S(1)} %get-tuple-element.1124), channel_id=1, source_target_pairs={{0,8},{8,16},{16,24},{24,32},{32,40},{40,48},{48,56},{56,64},{64,7... | collective-permute-start | bytes 13832 | tf_op jit(solution)/shard_map/ppermute | solution.py:15
  170.4 23.5 %collective-permute-start.27 = (f32[3,3,128]{2,1,0:T(4,128)S(1)}, f32[3,3,128]{2,1,0:T(4,128)S(1)}, u32[]{:S(2)}, u32[]{:S(2)}) collective-permute-start(f32[3,3,128]{2,1,0:T(4,128)S(1)} %get-tuple-element.1123), channel_id=1, source_target_pairs={{0,8},{8,16},{16,24},{24,32},{32,40},{40,48},{48,56},{56,64},{64,7... | collective-permute-start | bytes 13832 | tf_op jit(solution)/shard_map/ppermute | solution.py:15
  170.5 35.1 %collective-permute-start.29 = (f32[3,3,128]{2,1,0:T(4,128)S(1)}, f32[3,3,128]{2,1,0:T(4,128)S(1)}, u32[]{:S(2)}, u32[]{:S(2)}) collective-permute-start(f32[3,3,128]{2,1,0:T(4,128)S(1)} %get-tuple-element.1122), channel_id=1, source_target_pairs={{0,1},{1,2},{2,3},{3,4},{4,5},{5,6},{6,7},{8,9},{9,10},{10,11},{11... | collective-permute-start | bytes 13832 | tf_op jit(solution)/shard_map/ppermute | solution.py:21
  180.8 24.8 %collective-permute-start.30 = (f32[3,3,128]{2,1,0:T(4,128)S(1)}, f32[3,3,128]{2,1,0:T(4,128)S(1)}, u32[]{:S(2)}, u32[]{:S(2)}) collective-permute-start(f32[3,3,128]{2,1,0:T(4,128)S(1)} %get-tuple-element.1121), channel_id=1, source_target_pairs={{1,0},{2,1},{3,2},{4,3},{5,4},{6,5},{7,6},{9,8},{10,9},{11,10},{12... | collective-permute-start | bytes 13832 | tf_op jit(solution)/shard_map/ppermute | solution.py:21
  281.1 14.8 %collective-permute-start.37 = (f32[3,3,128]{2,1,0:T(4,128)S(1)}, f32[3,3,128]{2,1,0:T(4,128)S(1)}, u32[]{:S(2)}, u32[]{:S(2)}) collective-permute-start(f32[3,3,128]{2,1,0:T(4,128)S(1)} %collective-permute-done.36), channel_id=1, source_target_pairs={{0,1},{1,2},{2,3},{3,4},{4,5},{5,6},{6,7},{8,9},{9,10},{10,11},{11... | collective-permute-start | bytes 13832 | tf_op jit(solution)/shard_map/ppermute | solution.py:21
  291.4 10.8 %collective-permute-start.39 = (f32[3,3,128]{2,1,0:T(4,128)S(1)}, f32[3,3,128]{2,1,0:T(4,128)S(1)}, u32[]{:S(2)}, u32[]{:S(2)}) collective-permute-start(f32[3,3,128]{2,1,0:T(4,128)S(1)} %bitcast.331), channel_id=1, source_target_pairs={{0,8},{8,16},{16,24},{24,32},{32,40},{40,48},{48,56},{56,64},{64,7... | collective-permute-start | bytes 13832 | tf_op jit(solution)/shard_map/ppermute | solution.py:15
  291.5 21.8 %collective-permute-start.41 = (f32[3,3,128]{2,1,0:T(4,128)S(1)}, f32[3,3,128]{2,1,0:T(4,128)S(1)}, u32[]{:S(2)}, u32[]{:S(2)}) collective-permute-start(f32[3,3,128]{2,1,0:T(4,128)S(1)} %bitcast.330), channel_id=1, source_target_pairs={{0,1},{1,2},{2,3},{3,4},{4,5},{5,6},{6,7},{8,9},{9,10},{10,11},{11... | collective-permute-start | bytes 13832 | tf_op jit(solution)/shard_map/ppermute | solution.py:21
  293.4 19.9 %collective-permute-start.42 = (f32[3,3,128]{2,1,0:T(4,128)S(1)}, f32[3,3,128]{2,1,0:T(4,128)S(1)}, u32[]{:S(2)}, u32[]{:S(2)}) collective-permute-start(f32[3,3,128]{2,1,0:T(4,128)S(1)} %bitcast.329), channel_id=1, source_target_pairs={{1,0},{2,1},{3,2},{4,3},{5,4},{6,5},{7,6},{9,8},{10,9},{11,10},{12... | collective-permute-start | bytes 13832 | tf_op jit(solution)/shard_map/ppermute | solution.py:21
  389.2 15.1 %collective-permute-start.48 = (f32[3,3,128]{2,1,0:T(4,128)S(1)}, f32[3,3,128]{2,1,0:T(4,128)S(1)}, u32[]{:S(2)}, u32[]{:S(2)}) collective-permute-start(f32[3,3,128]{2,1,0:T(4,128)S(1)} %get-tuple-element.1109), channel_id=1, source_target_pairs={{0,8},{8,16},{16,24},{24,32},{32,40},{40,48},{48,56},{56,64},{64,7... | collective-permute-start | bytes 13832 | tf_op jit(solution)/shard_map/ppermute | solution.py:15
  391.4 21.8 %collective-permute-start.50 = (f32[3,3,128]{2,1,0:T(4,128)S(1)}, f32[3,3,128]{2,1,0:T(4,128)S(1)}, u32[]{:S(2)}, u32[]{:S(2)}) collective-permute-start(f32[3,3,128]{2,1,0:T(4,128)S(1)} %get-tuple-element.1108), channel_id=1, source_target_pairs={{0,8},{8,16},{16,24},{24,32},{32,40},{40,48},{48,56},{56,64},{64,7... | collective-permute-start | bytes 13832 | tf_op jit(solution)/shard_map/ppermute | solution.py:15
  391.5 23.4 %collective-permute-start.51 = (f32[3,3,128]{2,1,0:T(4,128)S(1)}, f32[3,3,128]{2,1,0:T(4,128)S(1)}, u32[]{:S(2)}, u32[]{:S(2)}) collective-permute-start(f32[3,3,128]{2,1,0:T(4,128)S(1)} %get-tuple-element.1107), channel_id=1, source_target_pairs={{0,8},{8,16},{16,24},{24,32},{32,40},{40,48},{48,56},{56,64},{64,7... | collective-permute-start | bytes 13832 | tf_op jit(solution)/shard_map/ppermute | solution.py:15
  391.6 35.0 %collective-permute-start.53 = (f32[3,3,128]{2,1,0:T(4,128)S(1)}, f32[3,3,128]{2,1,0:T(4,128)S(1)}, u32[]{:S(2)}, u32[]{:S(2)}) collective-permute-start(f32[3,3,128]{2,1,0:T(4,128)S(1)} %get-tuple-element.1106), channel_id=1, source_target_pairs={{0,1},{1,2},{2,3},{3,4},{4,5},{5,6},{6,7},{8,9},{9,10},{10,11},{11... | collective-permute-start | bytes 13832 | tf_op jit(solution)/shard_map/ppermute | solution.py:21
  401.9 24.8 %collective-permute-start.54 = (f32[3,3,128]{2,1,0:T(4,128)S(1)}, f32[3,3,128]{2,1,0:T(4,128)S(1)}, u32[]{:S(2)}, u32[]{:S(2)}) collective-permute-start(f32[3,3,128]{2,1,0:T(4,128)S(1)} %get-tuple-element.1105), channel_id=1, source_target_pairs={{1,0},{2,1},{3,2},{4,3},{5,4},{6,5},{7,6},{9,8},{10,9},{11,10},{12... | collective-permute-start | bytes 13832 | tf_op jit(solution)/shard_map/ppermute | solution.py:21
  (42 other events, 428.8 us)
